TPU v7x, 32 devices: a whole 2x2x4 slice. The times are simulated.
32 devices in a mesh: row: 8 (over z, x), col: 4 (over y, core).
Axes of the slice: x: 2, y: 2, z: 4, core: 2. Of those that a mesh axis runs over, the one named last changes fastest.
Arguments:
- blocks: bfloat16 [8, 4, 256, 128, 128], P('row', 'col'), may hold values from -0.25 to 0.25
- block_rows: int32 [8, 4, 256], P('row', 'col'), may hold values from 0 to 255
- block_cols: int32 [8, 4, 256], P('row', 'col'), may hold values from 0 to 255
- counts: int32 [8, 4], P('row', 'col'), may hold values from 85 to 256, as said below
- data: float32 [262144], P('row'), may hold values from -16 to 16
Outputs:
- solution: float32 [131072], P('col')
- search: float32 [131072], P('col')
- data_basis: float32 [262144], P('row')
Inputs may be any that keep to these rules, and one draw needn't show every extreme that they name: `counts`: every tile has between 85 and 256 live slots; some tile has exactly 256.
All inputs are finite; a program needn't handle non-finite values.
Results may differ from a plain program's by a relative error of at most 0.013.
Values sent between devices are 32-bit elements; how exact they have to be, the bound alone decides.
No kernel may reach another device: no remote copies, remote signals or barrier semaphores. Data moves between devices by JAX's collectives and lax.ppermute only.
A program may use at most 64 MiB of HBM per device.

v0:
```python
import jax
import jax.numpy as jnp
from jax import lax
from jax.sharding import PartitionSpec as P

TILE_COLS = 256
ITERS = 3
EPS = 1e-06


def local_forward(tile_blocks, rows, cols, count, vector, tile_rows):
    width = tile_blocks.shape[-1]
    vec_b = vector.astype(jnp.bfloat16).reshape(-1, width)
    picked = jnp.take(vec_b, cols, axis=0)
    prod = jnp.einsum("kij,kj->ki", tile_blocks, picked, preferred_element_type=jnp.float32)
    live = (jnp.arange(tile_blocks.shape[0], dtype=jnp.int32) < count).astype(jnp.float32)
    prod = prod * live[:, None]
    return jax.ops.segment_sum(prod, rows, num_segments=tile_rows).reshape(-1)


def local_adjoint(tile_blocks, rows, cols, count, vector, tile_cols):
    width = tile_blocks.shape[-1]
    vec_b = vector.astype(jnp.bfloat16).reshape(-1, width)
    picked = jnp.take(vec_b, rows, axis=0)
    prod = jnp.einsum("kij,ki->kj", tile_blocks, picked, preferred_element_type=jnp.float32)
    live = (jnp.arange(tile_blocks.shape[0], dtype=jnp.int32) < count).astype(jnp.float32)
    prod = prod * live[:, None]
    return jax.ops.segment_sum(prod, cols, num_segments=tile_cols).reshape(-1)


def first_norm(data):
    return jnp.sqrt(lax.psum(jnp.sum(data * data), "row") + EPS)


def new_data_basis(partial_value, previous, alpha):
    summed = lax.psum(partial_value, "col")
    temp = summed - alpha * previous
    return (temp, None)


def new_model_basis(partial_value, previous, beta):
    summed = lax.psum(partial_value, "row")
    temp = summed - beta * previous
    alpha = jnp.sqrt(lax.psum(jnp.sum(temp * temp), "col") + EPS)
    return (temp / alpha, alpha)


def per_device(blocks, block_rows, block_cols, counts, data):
    tile_blocks = blocks[0, 0]
    rows = block_rows[0, 0]
    cols = block_cols[0, 0]
    count = counts[0, 0]
    width = tile_blocks.shape[-1]
    tile_rows = data.shape[0] // width
    tile_cols = TILE_COLS
    beta = first_norm(data)
    data_basis = data / beta
    zero_model = jnp.zeros((tile_cols * width,), jnp.float32)
    model_basis, alpha = new_model_basis(
        local_adjoint(tile_blocks, rows, cols, count, data_basis, tile_cols),
        zero_model,
        jnp.float32(0.0),
    )
    search = model_basis
    solution = zero_model
    phibar = beta
    rhobar = alpha
    for step in range(ITERS):
        partial_value = local_forward(tile_blocks, rows, cols, count, model_basis, tile_rows)
        temp, unused = new_data_basis(partial_value, data_basis, alpha)
        beta = first_norm(temp)
        data_basis = temp / beta
        partial_model = local_adjoint(tile_blocks, rows, cols, count, data_basis, tile_cols)
        model_basis, alpha = new_model_basis(partial_model, model_basis, beta)
        rho = jnp.sqrt(rhobar * rhobar + beta * beta)
        cosine = rhobar / rho
        sine = beta / rho
        theta = sine * alpha
        rhobar = -cosine * alpha
        phi = cosine * phibar
        phibar = sine * phibar
        solution = solution + phi / rho * search
        search = model_basis - theta / rho * search
    return (solution, search, data_basis)


def solution(mesh):
    in_specs = (
        P("row", "col", None, None, None),
        P("row", "col", None),
        P("row", "col", None),
        P("row", "col"),
        P("row"),
    )
    out_specs = (P("col"), P("col"), P("row"))
    return jax.shard_map(
        per_device, mesh=mesh, in_specs=in_specs, out_specs=out_specs, check_vma=False
    )
```

profile of v0, /device:TPU:0, one launch (start us, length us, event | category | flops | bytes accessed | tf_op | source)
XLA Modules:
  0.0 587.4 jit_solution(584488901513735829)
XLA Ops:
  10.8 23.8 %psum.105 = f32[]{:T(128)} all-reduce(f32[]{:T(128)} %multiply_reduce_fusion.7), channel_id=1, replica_groups=mesh['row'=8,'col'=4] {'row'}, use_global_device_ids=true, to_apply=%region_1.0 | all-reduce | flops 1 | bytes 8 | tf_op jit(solution)/shard_map/psum | solution.py:32
  37.2 5.7 fusion.12
  45.1 67.8 %all-reduce.8.cloned.1.call-done = f32[32768]{0:T(1024)} async-done(((f32[32768]{0:T(1024)}), f32[32768]{0:T(1024)}) %all-reduce.8.cloned.1.call-update) | async-done | bytes 131088 | tf_op jit(solution)/shard_map/psum | solution.py:42
  114.5 6.3 %psum.107 = f32[]{:T(128)} all-reduce(f32[]{:T(128)} %multiply_reduce_fusion.6), channel_id=1, replica_groups=mesh['row'=8,'col'=4] {'col'}, use_global_device_ids=true, to_apply=%region_5.7 | all-reduce | flops 1 | bytes 8 | tf_op jit(solution)/shard_map/psum | solution.py:44
  123.4 7.8 %fusion.10 = f32[256,1,128]{2,1,0:T(1,128)S(1)} fusion(bf16[1,1,256,128,128]{4,3,2,1,0:T(8,128)(2,1)} %param.7, bf16[256,128,1]{1,0,2:T(8,128)(2,1)S(1)} %select_bitcast_fusion.5), kind=kOutput, calls=%fused_computation.24 | convolution fusion | flops 8388608 | bytes 8585216 | tf_op jit(solution)/shard_map/kij,kj->ki/dot_general | solution.py:15
  131.2 2.3 scatter_custom_fusion.1
  133.5 31.3 %all-reduce.10.cloned.1.call-done = f32[32768]{0:T(1024)} async-done(((f32[32768]{0:T(1024)}), f32[32768]{0:T(1024)}) %all-reduce.10.cloned.1.call-update) | async-done | bytes 131088 | tf_op jit(solution)/shard_map/psum | solution.py:36
  166.4 22.0 %psum.109 = f32[]{:T(128)} all-reduce(f32[]{:T(128)} %get-tuple-element.10), channel_id=1, replica_groups=mesh['row'=8,'col'=4] {'row'}, use_global_device_ids=true, to_apply=%region_9.11 | all-reduce | flops 1 | bytes 8 | tf_op jit(solution)/shard_map/psum | solution.py:32
  190.0 5.7 fusion.8
  197.9 66.8 %all-reduce.12.cloned.1.call-done = f32[32768]{0:T(1024)} async-done(((f32[32768]{0:T(1024)}), f32[32768]{0:T(1024)}) %all-reduce.12.cloned.1.call-update) | async-done | bytes 131088 | tf_op jit(solution)/shard_map/psum | solution.py:42
  266.3 6.4 %psum.111 = f32[]{:T(128)} all-reduce(f32[]{:T(128)} %multiply_reduce_fusion.4), channel_id=1, replica_groups=mesh['row'=8,'col'=4] {'col'}, use_global_device_ids=true, to_apply=%region_13.15 | all-reduce | flops 1 | bytes 8 | tf_op jit(solution)/shard_map/psum | solution.py:44
  275.3 7.8 %fusion.6 = f32[256,1,128]{2,1,0:T(1,128)S(1)} fusion(bf16[1,1,256,128,128]{4,3,2,1,0:T(8,128)(2,1)} %param.7, bf16[256,128,1]{1,0,2:T(8,128)(2,1)S(1)} %select_bitcast_fusion.3), kind=kOutput, calls=%fused_computation.20 | convolution fusion | flops 8388608 | bytes 8585216 | tf_op jit(solution)/shard_map/kij,kj->ki/dot_general | solution.py:15
  283.1 2.3 scatter_custom_fusion.3
  285.5 31.3 %all-reduce.14.cloned.1.call-done = f32[32768]{0:T(1024)} async-done(((f32[32768]{0:T(1024)}), f32[32768]{0:T(1024)}) %all-reduce.14.cloned.1.call-update) | async-done | bytes 131088 | tf_op jit(solution)/shard_map/psum | solution.py:36
  318.3 22.0 %psum.113 = f32[]{:T(128)} all-reduce(f32[]{:T(128)} %get-tuple-element.6), channel_id=1, replica_groups=mesh['row'=8,'col'=4] {'row'}, use_global_device_ids=true, to_apply=%region_17.19 | all-reduce | flops 1 | bytes 8 | tf_op jit(solution)/shard_map/psum | solution.py:32
  341.9 5.7 fusion.4
  349.8 66.8 %all-reduce.16.cloned.1.call-done = f32[32768]{0:T(1024)} async-done(((f32[32768]{0:T(1024)}), f32[32768]{0:T(1024)}) %all-reduce.16.cloned.1.call-update) | async-done | bytes 131088 | tf_op jit(solution)/shard_map/psum | solution.py:42
  418.2 6.3 %psum.115 = f32[]{:T(128)} all-reduce(f32[]{:T(128)} %multiply_reduce_fusion.2), channel_id=1, replica_groups=mesh['row'=8,'col'=4] {'col'}, use_global_device_ids=true, to_apply=%region_21.23 | all-reduce | flops 1 | bytes 8 | tf_op jit(solution)/shard_map/psum | solution.py:44
  427.1 7.8 %fusion.2 = f32[256,1,128]{2,1,0:T(1,128)S(1)} fusion(bf16[1,1,256,128,128]{4,3,2,1,0:T(8,128)(2,1)} %param.7, bf16[256,128,1]{1,0,2:T(8,128)(2,1)S(1)} %select_bitcast_fusion.1), kind=kOutput, calls=%fused_computation.16 | convolution fusion | flops 8388608 | bytes 8585216 | tf_op jit(solution)/shard_map/kij,kj->ki/dot_general | solution.py:15
  437.2 31.3 %all-reduce.18.cloned.1.call-done = f32[32768]{0:T(1024)} async-done(((f32[32768]{0:T(1024)}), f32[32768]{0:T(1024)}) %all-reduce.18.cloned.1.call-update) | async-done | bytes 131088 | tf_op jit(solution)/shard_map/psum | solution.py:36
  470.0 22.2 %psum.117 = f32[]{:T(128)} all-reduce(f32[]{:T(128)} %multiply_reduce_fusion.1), channel_id=1, replica_groups=mesh['row'=8,'col'=4] {'row'}, use_global_device_ids=true, to_apply=%region_25.27 | all-reduce | flops 1 | bytes 8 | tf_op jit(solution)/shard_map/psum | solution.py:32
  495.5 5.7 fusion
  503.9 66.3 %all-reduce.20.cloned.1.call-done = f32[32768]{0:T(1024)} async-done(((f32[32768]{0:T(1024)}), f32[32768]{0:T(1024)}) %all-reduce.20.cloned.1.call-update) | async-done | bytes 131088 | tf_op jit(solution)/shard_map/psum | solution.py:42
  571.8 6.3 %psum.119 = f32[]{:T(128)} all-reduce(f32[]{:T(128)} %multiply_reduce_fusion), channel_id=1, replica_groups=mesh['row'=8,'col'=4] {'col'}, use_global_device_ids=true, to_apply=%region_29.31 | all-reduce | flops 1 | bytes 8 | tf_op jit(solution)/shard_map/psum | solution.py:44
  (64 shorter events, 38.8 us)
Async XLA Ops:
  7.2 35.7 %copy-start.3 = (s32[1,1,256]{2,1,0:T(1,128)S(1)}, s32[1,1,256]{2,1,0:T(1,128)}, u32[]{:S(2)}) copy-start(s32[1,1,256]{2,1,0:T(1,128)} %param.9) | copy-start | bytes 3076
  7.2 105.8 %all-reduce.8.cloned.1.call-start = ((), (), s32[]{:S(2)}) async-start(), calls=%async_computation | async-start | bytes 262144 | tf_op jit(solution)/shard_map/psum | solution.py:42
  37.2 127.6 %copy-start.2 = (f32[32768]{0:T(1024)S(1)}, f32[32768]{0:T(1024)}, u32[]{:S(2)}) copy-start(f32[32768]{0:T(1024)} %param.11) | copy-start | bytes 393220
  45.0 119.8 %all-reduce.10.cloned.1.call-start = ((), (), s32[]{:S(2)}) async-start(), calls=%async_computation.1 | async-start | bytes 262144 | tf_op jit(solution)/shard_map/psum | solution.py:36
  123.4 141.4 %copy-start = (f32[32768]{0:T(1024)S(1)}, f32[32768]{0:T(1024)}, u32[]{:S(2)}) copy-start(f32[32768]{0:T(1024)} %all-reduce.8.cloned.1.call-done) | copy-start | bytes 393220
  133.5 131.2 %all-reduce.12.cloned.1.call-start = ((), (), s32[]{:S(2)}) async-start(), calls=%async_computation.2 | async-start | bytes 262144 | tf_op jit(solution)/shard_map/psum | solution.py:42
  197.8 118.9 %all-reduce.14.cloned.1.call-start = ((), (), s32[]{:S(2)}) async-start(), calls=%async_computation.3 | async-start | bytes 262144 | tf_op jit(solution)/shard_map/psum | solution.py:36
  285.4 131.2 %all-reduce.16.cloned.1.call-start = ((), (), s32[]{:S(2)}) async-start(), calls=%async_computation.4 | async-start | bytes 262144 | tf_op jit(solution)/shard_map/psum | solution.py:42
  349.8 118.7 %all-reduce.18.cloned.1.call-start = ((), (), s32[]{:S(2)}) async-start(), calls=%async_computation.5 | async-start | bytes 262144 | tf_op jit(solution)/shard_map/psum | solution.py:36
  427.0 143.2 %copy-start.1 = (f32[32768]{0:T(1024)S(1)}, f32[32768]{0:T(1024)}, u32[]{:S(2)}) copy-start(f32[32768]{0:T(1024)} %all-reduce.16.cloned.1.call-done) | copy-start | bytes 393220
  437.2 133.0 %all-reduce.20.cloned.1.call-start = ((), (), s32[]{:S(2)}) async-start(), calls=%async_computation.6 | async-start | bytes 262144 | tf_op jit(solution)/shard_map/psum | solution.py:42
Sparse Core Ops, SparseCore 0:
  45.1 67.7 all-reduce.7
  133.6 31.1 all-reduce.9
  197.9 66.7 all-reduce.11
  285.5 31.1 all-reduce.13
  349.9 66.7 all-reduce.15
  437.3 31.1 all-reduce.17
  503.4 66.7 all-reduce.19
where the time goes:
time: 588 us; the launch traced here: 587 us
  waiting for transfers between devices  362 us (62%)
  blocking collectives  115 us (20%)
  matrix products  46 us (8%)
  other arithmetic  37 us (6%)
  between operations  21.2 us (4%)
  local copies, waits for them, and re-layouts  6.01 us (1%)
    psum x4, waiting for transfers between devices, new_model_basis(): summed = lax.psum(partial_value, 'row')  268 us
    psum x3, waiting for transfers between devices, new_data_basis(): summed = lax.psum(partial_value, 'col')  93.8 us
    psum x4, blocking collectives, first_norm(): return jnp.sqrt(lax.psum(jnp.sum(data * data), 'row') + EPS)  89.9 us
    psum x4, blocking collectives, new_model_basis(): alpha = jnp.sqrt(lax.psum(jnp.sum(temp * temp), 'col') + EPS)  25.3 us
    dot_general x3, matrix products, local_forward(): jnp.einsum('kij,kj->ki', tile_blocks, picked, preferred_element_type=jnp....  23.4 us
    dot_general x4, matrix products, local_adjoint(): jnp.einsum('kij,ki->kj', tile_blocks, picked, preferred_element_type=jnp....  22.6 us
  transfers between devices with their start and end apart: 7, of which 7 were waited for; matrix products, arithmetic and copies ran while one was open for 0% of the time, Pallas kernels for 0%

commit v1 on v0

--- a/solution.py
+++ b/solution.py
@@ -33,7 +33,8 @@
 
 
 def new_data_basis(partial_value, previous, alpha):
-    summed = lax.psum(partial_value, "col")
+    pieces = lax.all_gather(partial_value, "col", axis=0, tiled=False)
+    summed = pieces.sum(axis=0)
     temp = summed - alpha * previous
     return (temp, None)
 

time: 588 us -> 508 us (0.86)
  waiting for transfers between devices: 362 us -> 269 us
  blocking collectives: 115 us -> 132 us
    psum x3 -> x0, waiting for transfers between devices: 93.8 us -> none  [new_data_basis(): summed = lax.psum(partial_value, 'col')]
    all_gather x0 -> x3, blocking collectives: none -> 22.2 us  [new_data_basis(): pieces = lax.all_gather(partial_value, 'col', axis=0, tiled=False)]
  transfers between devices with their start and end apart: 7 -> 4, of which waited for: 7 -> 4; matrix products, arithmetic and copies ran while one was open for 0% -> 0% of each run, Pallas kernels for 0% -> 0%
where the time goes in v1:
time: 508 us; the launch traced here: 507 us
  waiting for transfers between devices  269 us (53%)
  blocking collectives  132 us (26%)
  matrix products  46 us (9%)
  other arithmetic  33.1 us (7%)
  between operations  20.8 us (4%)
  local copies, waits for them, and re-layouts  6.01 us (1%)
    psum x4, waiting for transfers between devices, new_model_basis(): summed = lax.psum(partial_value, 'row')  269 us
    psum x4, blocking collectives, first_norm(): return jnp.sqrt(lax.psum(jnp.sum(data * data), 'row') + EPS)  84.4 us
    psum x4, blocking collectives, new_model_basis(): alpha = jnp.sqrt(lax.psum(jnp.sum(temp * temp), 'col') + EPS)  25.3 us
    dot_general x3, matrix products, local_forward(): jnp.einsum('kij,kj->ki', tile_blocks, picked, preferred_element_type=jnp....  23.4 us
    dot_general x4, matrix products, local_adjoint(): jnp.einsum('kij,ki->kj', tile_blocks, picked, preferred_element_type=jnp....  22.6 us
    all_gather x3, blocking collectives, new_data_basis(): pieces = lax.all_gather(partial_value, 'col', axis=0, tiled=False)  22.2 us
  transfers between devices with their start and end apart: 4, of which 4 were waited for; matrix products, arithmetic and copies ran while one was open for 0% of the time, Pallas kernels for 0%

profile of v1, /device:TPU:0, one launch (start us, length us, event | category | flops | bytes accessed | tf_op | source)
XLA Modules:
  0.0 507.1 jit_solution(15202003990289084342)
XLA Ops:
  10.1 23.7 %psum.84 = f32[]{:T(128)} all-reduce(f32[]{:T(128)} %multiply_reduce_fusion.7), channel_id=1, replica_groups=mesh['row'=8,'col'=4] {'row'}, use_global_device_ids=true, to_apply=%region_1.0 | all-reduce | flops 1 | bytes 8 | tf_op jit(solution)/shard_map/psum | solution.py:32
  37.1 5.7 %fusion.12 = f32[256,1,128]{2,1,0:T(1,128)S(1)} fusion(bf16[1,1,256,128,128]{4,3,2,1,0:T(8,128)(2,1)} %param.7, bf16[256,128,1]{1,0,2:T(8,128)(2,1)S(1)} %select_bitcast_fusion.6), kind=kOutput, calls=%fused_computation.26 | convolution fusion | flops 8388608 | bytes 8585216 | tf_op jit(solution)/shard_map/kij,ki->kj/dot_general | solution.py:25
  42.8 2.1 scatter_custom_fusion
  45.1 67.8 %all-reduce.5.cloned.1.call-done = f32[32768]{0:T(1024)} async-done(((f32[32768]{0:T(1024)}), f32[32768]{0:T(1024)}) %all-reduce.5.cloned.1.call-update) | async-done | bytes 131088 | tf_op jit(solution)/shard_map/psum | solution.py:43
  114.5 6.3 %psum.86 = f32[]{:T(128)} all-reduce(f32[]{:T(128)} %multiply_reduce_fusion.6), channel_id=1, replica_groups=mesh['row'=8,'col'=4] {'col'}, use_global_device_ids=true, to_apply=%region_5.7 | all-reduce | flops 1 | bytes 8 | tf_op jit(solution)/shard_map/psum | solution.py:45
  123.3 7.8 %fusion.10 = f32[256,1,128]{2,1,0:T(1,128)S(1)} fusion(bf16[1,1,256,128,128]{4,3,2,1,0:T(8,128)(2,1)} %param.7, bf16[256,128,1]{1,0,2:T(8,128)(2,1)S(1)} %select_bitcast_fusion.5), kind=kOutput, calls=%fused_computation.24 | convolution fusion | flops 8388608 | bytes 8585216 | tf_op jit(solution)/shard_map/kij,kj->ki/dot_general | solution.py:15
  132.9 7.4 %all-gather = f32[4,1,32768]{2,1,0:T(1,128)S(1)} all-gather(f32[1,1,32768]{2,1,0:T(1,128)S(1)} %bitcast.75), channel_id=1, replica_groups=mesh['row'=8,'col'=4] {'col'}, dimensions={0}, use_global_device_ids=true | all-gather | bytes 655360 | tf_op jit(solution)/shard_map/all_gather | solution.py:36
  141.4 20.2 %psum.87 = f32[]{:T(128)} all-reduce(f32[]{:T(128)} %get-tuple-element.10), channel_id=1, replica_groups=mesh['row'=8,'col'=4] {'row'}, use_global_device_ids=true, to_apply=%region_9.11 | all-reduce | flops 1 | bytes 8 | tf_op jit(solution)/shard_map/psum | solution.py:32
  163.3 5.7 %fusion.8 = f32[256,1,128]{2,1,0:T(1,128)S(1)} fusion(bf16[1,1,256,128,128]{4,3,2,1,0:T(8,128)(2,1)} %param.7, bf16[256,128,1]{1,0,2:T(8,128)(2,1)S(1)} %select_bitcast_fusion.4), kind=kOutput, calls=%fused_computation.22 | convolution fusion | flops 8388608 | bytes 8585216 | tf_op jit(solution)/shard_map/kij,ki->kj/dot_general | solution.py:25
  171.1 67.2 %all-reduce.7.cloned.1.call-done = f32[32768]{0:T(1024)} async-done(((f32[32768]{0:T(1024)}), f32[32768]{0:T(1024)}) %all-reduce.7.cloned.1.call-update) | async-done | bytes 131088 | tf_op jit(solution)/shard_map/psum | solution.py:43
  239.9 6.4 %psum.89 = f32[]{:T(128)} all-reduce(f32[]{:T(128)} %multiply_reduce_fusion.4), channel_id=1, replica_groups=mesh['row'=8,'col'=4] {'col'}, use_global_device_ids=true, to_apply=%region_13.15 | all-reduce | flops 1 | bytes 8 | tf_op jit(solution)/shard_map/psum | solution.py:45
  249.0 7.8 %fusion.6 = f32[256,1,128]{2,1,0:T(1,128)S(1)} fusion(bf16[1,1,256,128,128]{4,3,2,1,0:T(8,128)(2,1)} %param.7, bf16[256,128,1]{1,0,2:T(8,128)(2,1)S(1)} %select_bitcast_fusion.3), kind=kOutput, calls=%fused_computation.20 | convolution fusion | flops 8388608 | bytes 8585216 | tf_op jit(solution)/shard_map/kij,kj->ki/dot_general | solution.py:15
  258.5 7.4 %all-gather.1 = f32[4,1,32768]{2,1,0:T(1,128)S(1)} all-gather(f32[1,1,32768]{2,1,0:T(1,128)S(1)} %bitcast.76), channel_id=1, replica_groups=mesh['row'=8,'col'=4] {'col'}, dimensions={0}, use_global_device_ids=true | all-gather | bytes 655360 | tf_op jit(solution)/shard_map/all_gather | solution.py:36
  267.0 20.2 %psum.90 = f32[]{:T(128)} all-reduce(f32[]{:T(128)} %get-tuple-element.6), channel_id=1, replica_groups=mesh['row'=8,'col'=4] {'row'}, use_global_device_ids=true, to_apply=%region_17.19 | all-reduce | flops 1 | bytes 8 | tf_op jit(solution)/shard_map/psum | solution.py:32
  288.9 5.7 %fusion.4 = f32[256,1,128]{2,1,0:T(1,128)S(1)} fusion(bf16[1,1,256,128,128]{4,3,2,1,0:T(8,128)(2,1)} %param.7, bf16[256,128,1]{1,0,2:T(8,128)(2,1)S(1)} %select_bitcast_fusion.2), kind=kOutput, calls=%fused_computation.18 | convolution fusion | flops 8388608 | bytes 8585216 | tf_op jit(solution)/shard_map/kij,ki->kj/dot_general | solution.py:25
  294.5 2.1 scatter_custom_fusion.4
  296.7 67.2 %all-reduce.9.cloned.1.call-done = f32[32768]{0:T(1024)} async-done(((f32[32768]{0:T(1024)}), f32[32768]{0:T(1024)}) %all-reduce.9.cloned.1.call-update) | async-done | bytes 131088 | tf_op jit(solution)/shard_map/psum | solution.py:43
  365.5 6.3 %psum.92 = f32[]{:T(128)} all-reduce(f32[]{:T(128)} %multiply_reduce_fusion.2), channel_id=1, replica_groups=mesh['row'=8,'col'=4] {'col'}, use_global_device_ids=true, to_apply=%region_21.23 | all-reduce | flops 1 | bytes 8 | tf_op jit(solution)/shard_map/psum | solution.py:45
  374.4 7.8 %fusion.2 = f32[256,1,128]{2,1,0:T(1,128)S(1)} fusion(bf16[1,1,256,128,128]{4,3,2,1,0:T(8,128)(2,1)} %param.7, bf16[256,128,1]{1,0,2:T(8,128)(2,1)S(1)} %select_bitcast_fusion.1), kind=kOutput, calls=%fused_computation.16 | convolution fusion | flops 8388608 | bytes 8585216 | tf_op jit(solution)/shard_map/kij,kj->ki/dot_general | solution.py:15
  383.9 7.4 %all-gather.2 = f32[4,1,32768]{2,1,0:T(1,128)S(1)} all-gather(f32[1,1,32768]{2,1,0:T(1,128)S(1)} %bitcast.77), channel_id=1, replica_groups=mesh['row'=8,'col'=4] {'col'}, dimensions={0}, use_global_device_ids=true | all-gather | bytes 655360 | tf_op jit(solution)/shard_map/all_gather | solution.py:36
  392.4 20.4 %psum.93 = f32[]{:T(128)} all-reduce(f32[]{:T(128)} %multiply_reduce_fusion.1), channel_id=1, replica_groups=mesh['row'=8,'col'=4] {'row'}, use_global_device_ids=true, to_apply=%region_25.27 | all-reduce | flops 1 | bytes 8 | tf_op jit(solution)/shard_map/psum | solution.py:32
  415.2 5.7 %fusion = f32[256,1,128]{2,1,0:T(1,128)S(1)} fusion(bf16[1,1,256,128,128]{4,3,2,1,0:T(8,128)(2,1)} %param.7, bf16[256,128,1]{1,0,2:T(8,128)(2,1)S(1)} %select_bitcast_fusion), kind=kOutput, calls=%fused_computation.14 | convolution fusion | flops 8388608 | bytes 8585216 | tf_op jit(solution)/shard_map/kij,ki->kj/dot_general | solution.py:25
  423.6 66.7 %all-reduce.11.cloned.1.call-done = f32[32768]{0:T(1024)} async-done(((f32[32768]{0:T(1024)}), f32[32768]{0:T(1024)}) %all-reduce.11.cloned.1.call-update) | async-done | bytes 131088 | tf_op jit(solution)/shard_map/psum | solution.py:43
  491.9 6.3 %psum.95 = f32[]{:T(128)} all-reduce(f32[]{:T(128)} %multiply_reduce_fusion), channel_id=1, replica_groups=mesh['row'=8,'col'=4] {'col'}, use_global_device_ids=true, to_apply=%region_29.31 | all-reduce | flops 1 | bytes 8 | tf_op jit(solution)/shard_map/psum | solution.py:45
  (61 shorter events, 35.0 us)
Async XLA Ops:
  7.2 35.7 %copy-start.3 = (s32[1,1,256]{2,1,0:T(1,128)S(1)}, s32[1,1,256]{2,1,0:T(1,128)}, u32[]{:S(2)}) copy-start(s32[1,1,256]{2,1,0:T(1,128)} %param.9) | copy-start | bytes 3076
  7.2 105.7 %all-reduce.5.cloned.1.call-start = ((), (), s32[]{:S(2)}) async-start(), calls=%async_computation | async-start | bytes 262144 | tf_op jit(solution)/shard_map/psum | solution.py:43
  37.1 103.6 %copy-start.2 = (f32[32768]{0:T(1024)S(1)}, f32[32768]{0:T(1024)}, u32[]{:S(2)}) copy-start(f32[32768]{0:T(1024)} %param.11) | copy-start | bytes 393220
  45.0 193.4 %all-reduce.7.cloned.1.call-start = ((), (), s32[]{:S(2)}) async-start(), calls=%async_computation.1 | async-start | bytes 262144 | tf_op jit(solution)/shard_map/psum | solution.py:43
  123.3 115.1 %copy-start = (f32[32768]{0:T(1024)S(1)}, f32[32768]{0:T(1024)}, u32[]{:S(2)}) copy-start(f32[32768]{0:T(1024)} %all-reduce.5.cloned.1.call-done) | copy-start | bytes 393220
  171.1 192.9 %all-reduce.9.cloned.1.call-start = ((), (), s32[]{:S(2)}) async-start(), calls=%async_computation.2 | async-start | bytes 262144 | tf_op jit(solution)/shard_map/psum | solution.py:43
  296.7 193.6 %all-reduce.11.cloned.1.call-start = ((), (), s32[]{:S(2)}) async-start(), calls=%async_computation.3 | async-start | bytes 262144 | tf_op jit(solution)/shard_map/psum | solution.py:43
  374.4 115.9 %copy-start.1 = (f32[32768]{0:T(1024)S(1)}, f32[32768]{0:T(1024)}, u32[]{:S(2)}) copy-start(f32[32768]{0:T(1024)} %all-reduce.9.cloned.1.call-done) | copy-start | bytes 393220
Sparse Core Ops, SparseCore 0:
  45.1 67.7 all-reduce.4
  171.2 67.1 all-reduce.6
  296.8 67.0 all-reduce.8
  423.1 67.1 all-reduce.10
